TPU v7x, 32 devices: a whole 2x2x4 slice. The times are simulated.
32 devices in a mesh: dp: 8 (over y, x, core), mp: 4 (over z).
Axes of the slice: x: 2, y: 2, z: 4, core: 2. Of those that a mesh axis runs over, the one named last changes fastest.
Arguments:
- frames: bfloat16 [16384, 640], P('dp'), may hold values from -6 to 6
- seg_ids: int32 [16384], P('dp'), may hold values from 0 to 15, as said below
- qkv_weight: bfloat16 [3, 640, 768], P(None, 'dp', 'mp'), may hold values from -0.25 to 0.25
- qkv_bias: float32 [2, 768], P(None, 'mp'), may hold values from -3 to 3
- out_weight: bfloat16 [768, 640], P('mp', 'dp'), may hold values from -1.5 to 1.5
- out_bias: float32 [640], replicated, may hold values from -3 to 3
- gain_one: float32 [640], replicated, may hold values from 0.1 to 1.9
- shift_one: float32 [640], replicated, may hold values from -3 to 3
- up_weight: bfloat16 [640, 2240], P('dp', 'mp'), may hold values from -0.25 to 0.25
- up_bias: float32 [2240], P('mp'), may hold values from -3 to 3
- down_weight: bfloat16 [2240, 640], P('mp', 'dp'), may hold values from -0.125 to 0.125
- down_bias: float32 [640], replicated, may hold values from -3 to 3
- gain_two: float32 [640], replicated, may hold values from 0.1 to 1.9
- shift_two: float32 [640], replicated, may hold values from -3 to 3
- cotangent: bfloat16 [16384, 640], P('dp'), may hold values from -6 to 6
Outputs:
- output_frames: bfloat16 [16384, 640], P(('dp', 'mp'))
- frames_grad: bfloat16 [16384, 640], P(('dp', 'mp'))
- qkv_grad: float32 [3, 640, 768], P(None, 'dp', 'mp')
- qkv_bias_grad: float32 [2, 768], P(None, 'mp')
- out_grad: float32 [768, 640], P('mp', 'dp')
- out_bias_grad: float32 [640], replicated
- gain_one_grad: float32 [640], replicated
- shift_one_grad: float32 [640], replicated
- up_grad: float32 [640, 2240], P('dp', 'mp')
- up_bias_grad: float32 [2240], P('mp')
- down_grad: float32 [2240, 640], P('mp', 'dp')
- down_bias_grad: float32 [640], replicated
- gain_two_grad: float32 [640], replicated
- shift_two_grad: float32 [640], replicated
Inputs may be any that keep to these rules, and one draw needn't show every extreme that they name: `seg_ids`: each block of 2048 frames that one index of dp holds contains 1 to 16 whole utterances laid end to end; within the block the number starts at 0 and rises by one at each new utterance. In every draw some block holds a single utterance of 2048 frames and some block holds 16 utterances.
All inputs are finite; a program needn't handle non-finite values.
Results may differ from a plain program's by a relative error of at most 0.019.
Values may be sent and summed in bfloat16 or wider, within the bound.
A program may use at most 192 MiB of HBM per device.

v0:
```python
import jax
import jax.numpy as jnp
from jax import lax
from jax.sharding import PartitionSpec as P

HEADS = 10
HD = 64
EPS = 1e-05
SCALE = 0.125


def cut_along(array, dim, length):
    before, after = (array.shape[:dim], array.shape[dim + 1 :])
    return jnp.moveaxis(array.reshape(*before, length, -1, *after), dim, 0)


def sum_at_owner(array, axis, dim):
    parts = cut_along(array, dim, lax.axis_size(axis))
    arrived = lax.all_to_all(parts, axis, split_axis=0, concat_axis=0, tiled=True)
    return arrived.astype(jnp.float32).sum(axis=0)


def norm_forward(summed):
    centre = summed - jnp.mean(summed, -1, keepdims=True)
    spread = jnp.mean(centre * centre, -1, keepdims=True)
    factor = lax.rsqrt(spread + EPS)
    return (centre * factor, factor)


def norm_backward(upper, normed, factor, gain):
    scaled = upper * gain
    return factor * (
        scaled
        - jnp.mean(scaled, -1, keepdims=True)
        - normed * jnp.mean(scaled * normed, -1, keepdims=True)
    )


def gelu_exact(values):
    return jax.nn.gelu(values, approximate=False)


def body(
    frames,
    seg_ids,
    qkv_weight,
    qkv_bias,
    out_weight,
    out_bias,
    gain_one,
    shift_one,
    up_weight,
    up_bias,
    down_weight,
    down_bias,
    gain_two,
    shift_two,
    cotangent,
):
    qkv_full, out_full, up_full, down_full = (
        lax.all_gather(qkv_weight, "dp", axis=1, tiled=True),
        lax.all_gather(out_weight, "dp", axis=1, tiled=True),
        lax.all_gather(up_weight, "dp", axis=0, tiled=True),
        lax.all_gather(down_weight, "dp", axis=1, tiled=True),
    )
    total_rows = frames.shape[0]
    mp_size = lax.axis_size("mp")
    mp_index = lax.axis_index("mp")
    share_rows = total_rows // mp_size
    share_start = mp_index * share_rows
    slot_count = qkv_weight.shape[2] // HD
    hidden_cols = up_weight.shape[1]
    live_count = HEADS // mp_size + (mp_index < HEADS % mp_size).astype(jnp.int32)
    live_mask = (jnp.arange(slot_count) < live_count).astype(jnp.float32)
    live_low = live_mask.astype(jnp.bfloat16)
    projected = jnp.einsum("rd,ids->irs", frames, qkv_full, preferred_element_type=jnp.float32)
    offsets = jnp.stack([qkv_bias[0], jnp.zeros_like(qkv_bias[0]), qkv_bias[1]])
    head_values = (
        (projected + offsets[:, None, :])
        .astype(jnp.bfloat16)
        .reshape(3, total_rows, slot_count, HD)
    )
    queries = head_values[0]
    keys_all = head_values[1]
    values = head_values[2]
    block_rows = min(512, total_rows)
    block_count = total_rows // block_rows

    def scores_at(anchor):
        query_block = lax.dynamic_slice_in_dim(queries, anchor, block_rows, 0)
        seg_block = lax.dynamic_slice_in_dim(seg_ids, anchor, block_rows, 0)
        raw_scores = (
            jnp.einsum("qhd,khd->hqk", query_block, keys_all, preferred_element_type=jnp.float32)
            * SCALE
        )
        same_utter = seg_block[:, None] == seg_ids[None, :]
        return (query_block, jnp.where(same_utter[None], raw_scores, -1e30))

    def attend(position):
        unused, scores = scores_at(position * block_rows)
        maxima = jnp.max(scores, -1, keepdims=True)
        raised = jnp.exp(scores - maxima)
        totals = jnp.sum(raised, -1, keepdims=True)
        prob_low = (raised / totals).astype(jnp.bfloat16)
        mixed = jnp.einsum("hqk,khd->qhd", prob_low, values, preferred_element_type=jnp.float32)
        return (mixed, maxima, totals)

    attended, all_maxima, all_totals = lax.map(attend, jnp.arange(block_count))
    attended = attended.reshape(total_rows, slot_count, HD) * live_mask[None, :, None]
    mixed_low = attended.reshape(total_rows, slot_count * HD).astype(jnp.bfloat16)
    frames_wide = frames.astype(jnp.float32)

    def share_of(array):
        return lax.dynamic_slice_in_dim(array, share_start, share_rows, 0)

    attention = lax.psum(
        jnp.dot(mixed_low, out_full, preferred_element_type=jnp.float32).astype(jnp.bfloat16), "mp"
    ).astype(jnp.float32)
    normed_one, factor_one = norm_forward(frames_wide + attention + out_bias)
    hidden = normed_one * gain_one + shift_one
    hidden_low = hidden.astype(jnp.bfloat16)
    act_low = gelu_exact(
        jnp.dot(hidden_low, up_full, preferred_element_type=jnp.float32) + up_bias
    ).astype(jnp.bfloat16)
    feed = lax.psum(
        jnp.dot(act_low, down_full, preferred_element_type=jnp.float32).astype(jnp.bfloat16), "mp"
    ).astype(jnp.float32)
    normed_two, factor_two = norm_forward(hidden + feed + down_bias)
    output_frames = share_of(normed_two * gain_two + shift_two).astype(jnp.bfloat16)
    upstream = cotangent.astype(jnp.float32)
    sum_two_grad = norm_backward(upstream, normed_two, factor_two, gain_two)
    sum_two_low = sum_two_grad.astype(jnp.bfloat16)
    pre_act = jnp.dot(hidden_low, up_full, preferred_element_type=jnp.float32) + up_bias
    activation, pullback = jax.vjp(gelu_exact, pre_act)
    act_low = activation.astype(jnp.bfloat16)
    grad_down = jnp.einsum("rf,rd->fd", act_low, sum_two_low, preferred_element_type=jnp.float32)
    act_grad = jnp.einsum("rd,fd->rf", sum_two_low, down_full, preferred_element_type=jnp.float32)
    pre_low = pullback(act_grad)[0].astype(jnp.bfloat16)
    grad_up = jnp.einsum("rd,rf->df", hidden_low, pre_low, preferred_element_type=jnp.float32)
    bias_up = jnp.sum(pre_low.astype(jnp.float32), 0)
    grad_up, bias_up, grad_down, pre_low = (grad_up, bias_up, grad_down, pre_low)
    hidden_part = jnp.einsum("rf,df->rd", pre_low, up_full, preferred_element_type=jnp.float32)
    hidden_grad = (
        lax.psum(hidden_part.astype(jnp.bfloat16), "mp").astype(jnp.float32) + sum_two_grad
    )
    sum_one_grad = norm_backward(hidden_grad, normed_one, factor_one, gain_one)
    sum_one_low = sum_one_grad.astype(jnp.bfloat16)
    grad_proj = jnp.einsum("rs,rd->sd", mixed_low, sum_one_low, preferred_element_type=jnp.float32)
    back_mixed = jnp.einsum("rd,sd->rs", sum_one_low, out_full, preferred_element_type=jnp.float32)
    back_mixed = (
        back_mixed.astype(jnp.bfloat16).reshape(total_rows, slot_count, HD)
        * live_low[None, :, None]
    )

    def step(running, record):
        key_grad, value_grad = running
        position, maxima, totals = record
        anchor = position * block_rows
        query_block, scores = scores_at(anchor)
        probs = jnp.exp(scores - maxima) / totals
        prob_low = probs.astype(jnp.bfloat16)
        back_block = lax.dynamic_slice_in_dim(back_mixed, anchor, block_rows, 0)
        value_grad = value_grad + jnp.einsum(
            "hqk,qhd->khd", prob_low, back_block, preferred_element_type=jnp.float32
        )
        prob_grad = jnp.einsum(
            "qhd,khd->hqk", back_block, values, preferred_element_type=jnp.float32
        )
        score_low = (probs * (prob_grad - jnp.sum(probs * prob_grad, -1, keepdims=True))).astype(
            jnp.bfloat16
        )
        query_grad = (
            jnp.einsum("hqk,khd->qhd", score_low, keys_all, preferred_element_type=jnp.float32)
            * SCALE
        )
        key_grad = (
            key_grad
            + jnp.einsum("hqk,qhd->khd", score_low, query_block, preferred_element_type=jnp.float32)
            * SCALE
        )
        return ((key_grad, value_grad), query_grad)

    zeros = jnp.zeros((total_rows, slot_count, HD), jnp.float32)
    (key_grad, value_grad), query_grad = lax.scan(
        step, (zeros, zeros), (jnp.arange(block_count), all_maxima, all_totals)
    )
    query_grad = query_grad.reshape(total_rows, slot_count, HD)
    grads_low = (
        jnp.stack([query_grad, key_grad, value_grad])
        .reshape(3, total_rows, slot_count * HD)
        .astype(jnp.bfloat16)
    )
    grad_qkv = jnp.einsum("rd,irs->ids", frames, grads_low, preferred_element_type=jnp.float32)
    bias_qkv = jnp.stack(
        [jnp.sum(grads_low[0].astype(jnp.float32), 0), jnp.sum(grads_low[2].astype(jnp.float32), 0)]
    )
    grad_qkv, bias_qkv, grad_proj, grads_low = (grad_qkv, bias_qkv, grad_proj, grads_low)
    input_part = jnp.einsum("irs,ids->rd", grads_low, qkv_full, preferred_element_type=jnp.float32)
    input_grad = lax.psum(input_part.astype(jnp.bfloat16), "mp").astype(jnp.float32) + sum_one_grad
    frames_grad = share_of(input_grad).astype(jnp.bfloat16)
    upstream_share = share_of(upstream)
    hidden_share = share_of(hidden_grad)
    out_bias_term = jnp.sum(share_of(sum_one_low).astype(jnp.float32), 0)
    gain_one_term = jnp.sum(hidden_share * share_of(normed_one), 0)
    shift_one_term = jnp.sum(hidden_share, 0)
    down_bias_term = jnp.sum(share_of(sum_two_low).astype(jnp.float32), 0)
    gain_two_term = jnp.sum(upstream_share * share_of(normed_two), 0)
    shift_two_term = jnp.sum(upstream_share, 0)
    matrix_grads = (
        sum_at_owner(grad_qkv.astype(jnp.bfloat16), "dp", 1),
        sum_at_owner(grad_proj.astype(jnp.bfloat16), "dp", 1),
        sum_at_owner(grad_up.astype(jnp.bfloat16), "dp", 0),
        sum_at_owner(grad_down.astype(jnp.bfloat16), "dp", 1),
    )
    slot_width = slot_count * HD
    padded_qkv = lax.dynamic_update_slice(
        jnp.zeros((2, mp_size * slot_width), jnp.float32), bias_qkv, (0, mp_index * slot_width)
    )
    padded_up = lax.dynamic_update_slice(
        jnp.zeros((mp_size * hidden_cols,), jnp.float32), bias_up, (mp_index * hidden_cols,)
    )
    summed = lax.psum(
        (
            padded_qkv,
            padded_up,
            out_bias_term,
            gain_one_term,
            shift_one_term,
            down_bias_term,
            gain_two_term,
            shift_two_term,
        ),
        ("dp", "mp"),
    )
    qkv_bias_grad = lax.dynamic_slice_in_dim(summed[0], mp_index * slot_width, slot_width, 1)
    up_bias_grad = lax.dynamic_slice_in_dim(summed[1], mp_index * hidden_cols, hidden_cols, 0)
    return (
        output_frames,
        frames_grad,
        matrix_grads[0],
        qkv_bias_grad,
        matrix_grads[1],
        summed[2],
        summed[3],
        summed[4],
        matrix_grads[2],
        up_bias_grad,
        matrix_grads[3],
        summed[5],
        summed[6],
        summed[7],
    )


def solution(mesh):
    in_specs = (
        P("dp", None),
        P("dp"),
        P(None, "dp", "mp"),
        P(None, "mp"),
        P("mp", "dp"),
        P(),
        P(),
        P(),
        P("dp", "mp"),
        P("mp"),
        P("mp", "dp"),
        P(),
        P(),
        P(),
        P("dp", None),
    )
    out_specs = (
        P(("dp", "mp"), None),
        P(("dp", "mp"), None),
        P(None, "dp", "mp"),
        P(None, "mp"),
        P("mp", "dp"),
        P(),
        P(),
        P(),
        P("dp", "mp"),
        P("mp"),
        P("mp", "dp"),
        P(),
        P(),
        P(),
    )
    return jax.shard_map(body, mesh=mesh, in_specs=in_specs, out_specs=out_specs, check_vma=False)
```

profile of v0, /device:TPU:0, one launch (start us, length us, event | category | flops | bytes accessed | tf_op | source)
XLA Modules:
  0.0 783.6 jit_solution(1316347857595142371)
XLA Ops:
  8.2 11.1 %all_gather.13 = bf16[192,640]{0,1:T(8,128)(2,1)S(1)} all-gather(bf16[192,80]{0,1:T(8,128)(2,1)} %param.23), channel_id=1, replica_groups=mesh['dp'=8,'mp'=4] {'dp'}, dimensions={1}, use_global_device_ids=true | all-gather | bytes 276480 | tf_op jit(solution)/shard_map/all_gather | solution.py:62
  19.3 10.8 %all_gather.12 = bf16[3,640,192]{2,1,0:T(8,128)(2,1)S(1)} all-gather(bf16[3,80,192]{2,1,0:T(8,128)(2,1)} %param.21), channel_id=1, replica_groups=mesh['dp'=8,'mp'=4] {'dp'}, dimensions={1}, use_global_device_ids=true | all-gather | bytes 829440 | tf_op jit(solution)/shard_map/all_gather | solution.py:61
  30.2 4.4 fusion.38
  35.3 124.3 %while.29 = (s32[]{:T(128)}, f32[4,512,3,64]{1,0,3,2:T(4,128)}, f32[4,3,512,1]{2,1,3,0:T(4,128)}, f32[4,3,512,1]{2,1,3,0:T(4,128)S(1)}, s32[4]{0:T(128)S(1)}, /*...) while((s32[]{:T(128)}, f32[4,512,3,64]{1,0,3,2:T(4,128)}, ...), condition=%wide.region_3.4_spmd, body=%wide.region_0.3_spmd.sunk | while | flops 844100608 | bytes 45756624 | solution.py:108
  37.3 6.0 fusion.104
  43.3 6.8 fusion.105
  50.1 6.7 fusion.106
  57.8 8.6 %dynamic_update_slice.30 = f32[4,512,3,64]{1,0,3,2:T(4,128)} dynamic-update-slice(f32[4,512,3,64]{1,0,3,2:T(4,128)} %get-tuple-element.413, f32[1,512,3,64]{1,0,3,2:T(1,128)S(1)} %copy.68, s32[]{:T(128)S(6)} %copy.77, s32[]{:T(128)} %constant.76.clone.1..sunk, s32[]{:T(128)} %constant.76.clone.1..sunk, s32[]{:T(128)} %constant.76.clone.1..sunk) | dynamic-update-slice | bytes 786436 | tf_op jit(solution)/shard_map/while/body/jit(dynamic_update_index_in_dim)/dynamic_update_slice | solution.py:108
  68.4 6.0 fusion.104
  74.4 6.8 fusion.105
  81.2 6.7 fusion.106
  88.9 8.6 %dynamic_update_slice.30 = f32[4,512,3,64]{1,0,3,2:T(4,128)} dynamic-update-slice(f32[4,512,3,64]{1,0,3,2:T(4,128)} %get-tuple-element.413, f32[1,512,3,64]{1,0,3,2:T(1,128)S(1)} %copy.68, s32[]{:T(128)S(6)} %copy.77, s32[]{:T(128)} %constant.76.clone.1..sunk, s32[]{:T(128)} %constant.76.clone.1..sunk, s32[]{:T(128)} %constant.76.clone.1..sunk) | dynamic-update-slice | bytes 786436 | tf_op jit(solution)/shard_map/while/body/jit(dynamic_update_index_in_dim)/dynamic_update_slice | solution.py:108
  99.5 6.0 fusion.104
  105.5 6.8 fusion.105
  112.3 6.7 fusion.106
  119.9 8.6 %dynamic_update_slice.30 = f32[4,512,3,64]{1,0,3,2:T(4,128)} dynamic-update-slice(f32[4,512,3,64]{1,0,3,2:T(4,128)} %get-tuple-element.413, f32[1,512,3,64]{1,0,3,2:T(1,128)S(1)} %copy.68, s32[]{:T(128)S(6)} %copy.77, s32[]{:T(128)} %constant.76.clone.1..sunk, s32[]{:T(128)} %constant.76.clone.1..sunk, s32[]{:T(128)} %constant.76.clone.1..sunk) | dynamic-update-slice | bytes 786436 | tf_op jit(solution)/shard_map/while/body/jit(dynamic_update_index_in_dim)/dynamic_update_slice | solution.py:108
  130.5 6.0 fusion.104
  136.6 6.8 fusion.105
  143.3 6.7 fusion.106
  151.0 8.6 %dynamic_update_slice.30 = f32[4,512,3,64]{1,0,3,2:T(4,128)} dynamic-update-slice(f32[4,512,3,64]{1,0,3,2:T(4,128)} %get-tuple-element.413, f32[1,512,3,64]{1,0,3,2:T(1,128)S(1)} %copy.68, s32[]{:T(128)S(6)} %copy.77, s32[]{:T(128)} %constant.76.clone.1..sunk, s32[]{:T(128)} %constant.76.clone.1..sunk, s32[]{:T(128)} %constant.76.clone.1..sunk) | dynamic-update-slice | bytes 786436 | tf_op jit(solution)/shard_map/while/body/jit(dynamic_update_index_in_dim)/dynamic_update_slice | solution.py:108
  166.6 11.7 %all_gather.14 = bf16[640,560]{1,0:T(8,128)(2,1)} all-gather(bf16[80,560]{1,0:T(8,128)(2,1)S(1)} %copy-done.29), channel_id=1, replica_groups=mesh['dp'=8,'mp'=4] {'dp'}, dimensions={0}, use_global_device_ids=true | all-gather | bytes 806400 | tf_op jit(solution)/shard_map/all_gather | solution.py:63
  178.3 11.1 %all_gather.15 = bf16[560,640]{0,1:T(8,128)(2,1)} all-gather(bf16[560,80]{0,1:T(8,128)(2,1)S(1)} %copy-done.30), channel_id=1, replica_groups=mesh['dp'=8,'mp'=4] {'dp'}, dimensions={1}, use_global_device_ids=true | all-gather | bytes 806400 | tf_op jit(solution)/shard_map/all_gather | solution.py:64
  189.4 81.7 %all-reduce.6.cloned.1.call-done = bf16[2048,640]{1,0:T(8,128)(2,1)} async-done(((bf16[2048,640]{1,0:T(8,128)(2,1)}), bf16[2048,640]{1,0:T(8,128)(2,1)}) %all-reduce.6.cloned.1.call-update) | async-done | bytes 2621456 | tf_op jit(solution)/shard_map/psum | solution.py:116
  271.0 3.6 fusion.37
  277.4 13.3 %multiply_convert_fusion.1 = (bf16[2048,560]{0,1:T(8,128)(2,1)S(1)}, f32[2048,560]{0,1:T(8,128)}, f32[2048,560]{0,1:T(8,128)}) fusion(f32[560]{0:T(1024)S(1)} %copy-done.44, bf16[640,560]{1,0:T(8,128)(2,1)S(1)} %copy-done.23, f32[2048,640]{1,0:T(8,128)S(1)} %subtract_multiply_fusion.3, f32[640]{0:T(1024)S(1)} %copy-done.36, f32[640]{0:T(1024)S(1)} %copy-done.31), kind=kOutput, calls=%fused_computation.61 | convolution fusion | flops 1547632640 | bytes 17435840 | tf_op jit(solution)/shard_map/dot_general | solution.py:123
  292.1 3.9 convolution_convert_fusion.1
  296.3 103.0 %all-reduce.8.cloned.1.call-done = bf16[2048,640]{1,0:T(8,128)(2,1)} async-done(((bf16[2048,640]{1,0:T(8,128)(2,1)}), bf16[2048,640]{1,0:T(8,128)(2,1)}) %all-reduce.8.cloned.1.call-update) | async-done | bytes 2621456 | tf_op jit(solution)/shard_map/psum | solution.py:125
  399.3 4.5 fusion.52
  403.9 3.5 multiply_reduce_fusion.3
  413.3 4.5 convert_reduce_fusion
  419.2 4.0 convolution_convert_fusion
  423.7 5.2 convolution_convert_fusion.5
  431.2 4.2 all-to-all-start.3
  435.9 90.5 %all-reduce.10.cloned.1.call-done = bf16[2048,640]{1,0:T(8,128)(2,1)} async-done(((bf16[2048,640]{1,0:T(8,128)(2,1)}), bf16[2048,640]{1,0:T(8,128)(2,1)}) %all-reduce.10.cloned.1.call-update) | async-done | bytes 2621456 | tf_op jit(solution)/shard_map/psum | solution.py:144
  526.4 7.0 multiply_reduce_fusion.5
  533.5 6.6 fusion.57
  543.7 114.9 %while.30 = (s32[]{:T(128)}, f32[2048,3,64]{0,2,1:T(8,128)S(1)}, f32[2048,3,64]{0,2,1:T(8,128)S(1)}, bf16[4,512,3,64]{1,3,2,0:T(8,128)(2,1)}, s32[4]{0:T(128)S(1...) while((s32[]{:T(128)}, f32[2048,3,64]{0,2,1:T(8,128)S(1)}, ...), condition=%wide.region_17.18_spmd.clone, body=%wide.region_15.17_spmd.clone.sunk | while | flops 2047834624 | bytes 118950256 | solution.py:184
  546.4 3.2 fusion.116
  549.6 7.7 multiply_reduce_fusion.10
  557.3 5.5 multiply_convert_fusion.6
  562.8 6.2 fusion.118
  575.1 3.2 fusion.116
  578.3 7.7 multiply_reduce_fusion.10
  586.0 5.5 multiply_convert_fusion.6
  591.5 6.2 fusion.118
  603.9 3.2 fusion.116
  607.1 7.7 multiply_reduce_fusion.10
  614.8 5.5 multiply_convert_fusion.6
  620.2 6.2 fusion.118
  632.6 3.2 fusion.116
  635.8 7.7 multiply_reduce_fusion.10
  643.5 5.5 multiply_convert_fusion.6
  649.0 6.2 fusion.118
  666.2 4.0 bitcast_convert_fusion
  670.3 4.5 convolution_convert_fusion.4
  676.0 3.8 all-to-all-start.2
  682.8 3.0 dynamic-slice_reduce_fusion
  687.8 5.0 all-to-all-done.2
  693.6 3.0 convolution_convert_fusion.6
  698.5 4.1 all-to-all-start.1
  702.6 5.1 fusion.46
  712.2 4.2 all-to-all-start
  721.3 44.5 %all-reduce = (f32[2,768]{1,0:T(2,128)S(1)}, f32[640]{0:T(1024)}, f32[640]{0:T(1024)}, f32[640]{0:T(1024)}, f32[2240]{0:T(1024)S(1)}, /*index=5*/f32[640]{0:T(1024)}, f32[640]{0:T(1024)}, f32[640]{0:T(1024)}) all-reduce(f32[2,768]{1,0:T(2,128)S(1)} %dynamic_update_slice.20, ...), channel_id=1, replica_groups=mesh['dp'=8,'mp'=4] {'dp','mp'}, use_global_device_ids=true, to_apply=%region_22.23 | all-reduce | flops 7616 | bytes 60928 | tf_op jit(solution)/shard_map/psum | solution.py:222
  770.9 3.6 all-reduce.12.cloned.1.call-done
  (248 shorter events, 91.4 us)
Async XLA Ops:
  7.2 263.9 %all-reduce.6.cloned.1.call-start = ((), (), s32[]{:S(2)}) async-start(), calls=%async_computation.4 | async-start | bytes 5242880 | tf_op jit(solution)/shard_map/psum | solution.py:116
  7.4 155.2 %copy-start.39 = (f32[192]{0:T(256)}, f32[192]{0:T(256)S(1)}, u32[]{:S(2)}) copy-start(f32[192]{0:T(256)S(1)} %mul.192) | copy-start | bytes 2308
  30.1 4.6 copy-start.21
  159.6 6.8 copy-start.2
  159.6 6.8 copy-start.5
  159.6 6.8 copy-start.15
  159.6 6.9 copy-start.29
  162.6 15.7 %copy-start.30 = (bf16[560,80]{0,1:T(8,128)(2,1)S(1)}, bf16[560,80]{0,1:T(8,128)(2,1)}, u32[]{:S(2)}) copy-start(bf16[560,80]{0,1:T(8,128)(2,1)} %param.29) | copy-start | bytes 268804
  162.6 108.5 %copy-start.38 = (f32[640]{0:T(1024)S(1)}, f32[640]{0:T(1024)}, u32[]{:S(2)}) copy-start(f32[640]{0:T(1024)} %param.24) | copy-start | bytes 7684
  166.5 232.8 %all-reduce.8.cloned.1.call-start = ((), (), s32[]{:S(2)}) async-start(), calls=%async_computation.5 | async-start | bytes 5242880 | tf_op jit(solution)/shard_map/psum | solution.py:125
  166.5 108.1 %copy-start.11 = (bf16[2048,640]{1,0:T(8,128)(2,1)S(1)}, bf16[2048,640]{1,0:T(8,128)(2,1)}, u32[]{:S(2)}) copy-start(bf16[2048,640]{1,0:T(8,128)(2,1)} %param.19) | copy-start | bytes 7864324
  271.0 3.6 copy-start.12
  277.3 13.3 %copy-start = (f32[2048,640]{1,0:T(8,128)}, f32[2048,640]{1,0:T(8,128)S(1)}, u32[]{:S(2)}) copy-start(f32[2048,640]{1,0:T(8,128)S(1)} %subtract_multiply_fusion.3) | copy-start | bytes 15728644
  277.3 14.8 %copy-start.25 = (bf16[560,640]{0,1:T(8,128)(2,1)S(1)}, bf16[560,640]{0,1:T(8,128)(2,1)}, u32[]{:S(2)}) copy-start(bf16[560,640]{0,1:T(8,128)(2,1)} %all_gather.15) | copy-start | bytes 2150404
  290.7 1.4 copy-start.45
  292.1 107.2 %copy-start.35 = (f32[640]{0:T(1024)S(1)}, f32[640]{0:T(1024)}, u32[]{:S(2)}) copy-start(f32[640]{0:T(1024)} %param.30) | copy-start | bytes 7684
  296.0 230.4 %all-reduce.10.cloned.1.call-start = ((), (), s32[]{:S(2)}) async-start(), calls=%async_computation.6 | async-start | bytes 5242880 | tf_op jit(solution)/shard_map/psum | solution.py:144
  399.3 4.6 copy-start.10
  399.3 8.1 %slice-start = ((s8[5242880]{0:T(1024)(128)(4,1)}), s8[1048576]{0:T(1024)(128)(4,1)S(1)}, s32[]{:S(2)}) async-start(s8[5242880]{0:T(1024)(128)(4,1)} %bitcast.122), calls=%async_computation.8 | async-start | bytes 2097152
  403.9 3.6 copy-start.3
  403.9 3.6 copy-start.33
  403.9 4.5 slice-start.1
  403.9 9.3 %slice-start.2 = ((s8[4587520]{0:T(1024)(128)(4,1)}), s8[4194304]{0:T(1024)(128)(4,1)S(1)}, s32[]{:S(2)}) async-start(s8[4587520]{0:T(1024)(128)(4,1)} %bitcast.141), calls=%async_computation.10 | async-start | bytes 8388608
  403.9 9.3 %slice-start.4 = ((s8[4587520]{0:T(1024)(128)(4,1)}), s8[4194304]{0:T(1024)(128)(4,1)S(1)}, s32[]{:S(2)}) async-start(s8[4587520]{0:T(1024)(128)(4,1)} %bitcast.143), calls=%async_computation.12 | async-start | bytes 8388608
  408.4 4.8 slice-start.3
  408.4 4.8 slice-start.5
  410.9 2.3 copy-start.1
  413.2 4.6 copy-start.14
  413.2 5.9 copy-start.24
  431.2 244.8 %all-to-all-start.3 = ((bf16[8,560,80]{1,2,0:T(8,128)(2,1)}), bf16[8,560,80]{1,2,0:T(8,128)(2,1)}, u32[]{:S(2)}, u32[]{:S(2)}) async-start(bf16[8,560,80]{1,2,0:T(8,128)(2,1)} %bitcast.130), calls=%async_computation.3 | async-start | bytes 1638400 | tf_op jit(solution)/shard_map/all_to_all | solution.py:19
  435.4 339.0 %all-reduce.12.cloned.1.call-start = ((), (), s32[]{:S(2)}) async-start(), calls=%async_computation.7 | async-start | bytes 5242880 | tf_op jit(solution)/shard_map/psum | solution.py:199
  533.4 6.6 copy-start.9
  533.4 9.2 %copy-start.43 = (bf16[3]{0:T(256)(128)(2,1)S(1)}, bf16[3]{0:T(256)(128)(2,1)}, u32[]{:S(2)}) copy-start(bf16[3]{0:T(256)(128)(2,1)} %fusion.55) | copy-start | bytes 22
  540.0 1.5 copy-start.7
  546.4 3.2 copy-start.6
  546.4 3.2 copy-start.16
  562.8 6.2 copy-start.26
  571.0 1.4 copy-start.27
  575.1 3.2 copy-start.6
  575.1 3.2 copy-start.16
  591.5 6.2 copy-start.26
  599.7 1.4 copy-start.27
  603.8 3.2 copy-start.6
  603.9 3.2 copy-start.16
  620.2 6.2 copy-start.26
  628.5 1.4 copy-start.27
  632.6 3.2 copy-start.6
  632.6 3.2 copy-start.16
  649.0 6.2 copy-start.26
  657.2 1.4 copy-start.27
  664.2 2.0 copy-start.22
  666.2 4.0 copy-start.32
  666.2 4.0 copy-start.37
  666.2 4.1 copy-start.47
  674.8 5.1 copy-start.4
  676.0 6.5 copy-start.42
  676.0 6.8 copy-start.34
  676.0 6.8 copy-start.41
  676.0 16.8 %all-to-all-start.2 = ((bf16[8,80,560]{2,1,0:T(8,128)(2,1)}), bf16[8,80,560]{2,1,0:T(8,128)(2,1)S(1)}, u32[]{:S(2)}, u32[]{:S(2)}) async-start(bf16[8,80,560]{2,1,0:T(8,128)(2,1)} %bitcast.21), calls=%async_computation.2 | async-start | bytes 1638400 | tf_op jit(solution)/shard_map/all_to_all | solution.py:19
  682.5 11.1 %copy-start.8 = (bf16[2048,640]{1,0:T(8,128)(2,1)S(1)}, bf16[2048,640]{1,0:T(8,128)(2,1)}, u32[]{:S(2)}) copy-start(bf16[2048,640]{1,0:T(8,128)(2,1)} %copy-done.7) | copy-start | bytes 7864324
  682.5 11.1 %copy-start.40 = (f32[192]{0:T(256)S(1)}, f32[192]{0:T(256)}, u32[]{:S(2)}) copy-start(f32[192]{0:T(256)} %copy-done.39) | copy-start | bytes 2308
  693.6 8.9 %copy-start.18 = (bf16[1,2048,192]{1,2,0:T(8,128)(2,1)S(1)}, bf16[1,2048,192]{1,2,0:T(8,128)(2,1)}, u32[]{:S(2)}) copy-start(bf16[1,2048,192]{1,2,0:T(8,128)(2,1)} %stack.24) | copy-start | bytes 2359300
  698.5 13.7 %all-to-all-start.1 = ((bf16[8,192,80]{1,2,0:T(8,128)(2,1)}), bf16[8,192,80]{1,2,0:T(8,128)(2,1)}, u32[]{:S(2)}, u32[]{:S(2)}) async-start(bf16[8,192,80]{1,2,0:T(8,128)(2,1)} %bitcast.136), calls=%async_computation.1 | async-start | bytes 655360 | tf_op jit(solution)/shard_map/all_to_all | solution.py:19
  712.2 56.7 %all-to-all-start = ((bf16[8,3,80,192]{3,2,1,0:T(8,128)(2,1)}), bf16[8,3,80,192]{3,2,1,0:T(8,128)(2,1)}, u32[]{:S(2)}, u32[]{:S(2)}) async-start(bf16[8,3,80,192]{3,2,1,0:T(8,128)(2,1)} %copy.39), calls=%async_computation | async-start | bytes 1966080 | tf_op jit(solution)/shard_map/all_to_all | solution.py:19
  (10 other events, 11.3 us)
Sparse Core Ops, SparseCore 0:
  166.6 104.4 all-reduce.5
  296.2 103.1 all-reduce.7
  423.3 103.1 all-reduce.9
  670.4 104.0 all-reduce.11
where the time goes:
time: 795 us; the launch traced here: 784 us
  waiting for transfers between devices  284 us (36%)
  matrix products  188 us (24%)
  other arithmetic  107 us (13%)
  blocking collectives  89.2 us (11%)
  local copies, waits for them, and re-layouts  77.6 us (10%)
  starting transfers between devices  17.1 us (2%)
  between operations  14.7 us (2%)
    psum x1, waiting for transfers between devices, body(): lax.psum(jnp.dot(act_low, down_full, preferred_element_type=jnp.float32)....  103 us
    psum x1, waiting for transfers between devices, body(): lax.psum(hidden_part.astype(jnp.bfloat16), 'mp').astype(jnp.float32)  90.5 us
    psum x1, waiting for transfers between devices, body(): lax.psum(jnp.dot(mixed_low, out_full, preferred_element_type=jnp.float32)...  81.7 us
    dot_general x8, matrix products, scores_at(): jnp.einsum('qhd,khd->hqk', query_block, keys_all, preferred_element_type=...  54.9 us
    psum x1, blocking collectives, body(): lax.psum((padded_qkv, padded_up, out_bias_term, gain_one_term, shift_one_...  44.5 us
    dynamic_update_slice x12, local copies, waits for them, and re-layouts, body(): attended, all_maxima, all_totals = lax.map(attend, jnp.arange(block_count))  38.5 us
    reduce_sum x4, other arithmetic, attend(): totals = jnp.sum(raised, -1, keepdims=True)  27 us
    dot_general x4, matrix products, attend(): jnp.einsum('hqk,khd->qhd', prob_low, values, preferred_element_type=jnp.f...  26.6 us
  transfers between devices with their start and end apart: 8, of which 5 were waited for; matrix products, arithmetic and copies ran while one was open for 23% of the time, Pallas kernels for 0%

commit v1 on v0

--- a/solution.py
+++ b/solution.py
@@ -113,8 +113,12 @@
     def share_of(array):
         return lax.dynamic_slice_in_dim(array, share_start, share_rows, 0)
 
-    attention = lax.psum(
-        jnp.dot(mixed_low, out_full, preferred_element_type=jnp.float32).astype(jnp.bfloat16), "mp"
+    attention = jnp.sum(
+        lax.all_gather(
+            jnp.dot(mixed_low, out_full, preferred_element_type=jnp.float32).astype(jnp.bfloat16),
+            "mp",
+        ),
+        axis=0,
     ).astype(jnp.float32)
     normed_one, factor_one = norm_forward(frames_wide + attention + out_bias)
     hidden = normed_one * gain_one + shift_one

time: 795 us -> 880 us (1.11)
  waiting for transfers between devices: 284 us -> 363 us
    all_gather x0 -> x1, waiting for transfers between devices: none -> 162 us  [body(): lax.all_gather(jnp.dot(mixed_low, out_full, preferred_element_type=jnp.fl...]
    psum x1 -> x0, waiting for transfers between devices: 81.7 us -> none  [body(): lax.psum(jnp.dot(mixed_low, out_full, preferred_element_type=jnp.float32)...]
  transfers between devices with their start and end apart: 8 -> 8, of which waited for: 5 -> 5; matrix products, arithmetic and copies ran while one was open for 23% -> 21% of each run, Pallas kernels for 0% -> 0%
where the time goes in v1:
time: 880 us; the launch traced here: 869 us
  waiting for transfers between devices  363 us (41%)
  matrix products  188 us (21%)
  other arithmetic  114 us (13%)
  blocking collectives  89.2 us (10%)
  local copies, waits for them, and re-layouts  77.4 us (9%)
  starting transfers between devices  17.1 us (2%)
  between operations  14.7 us (2%)
    all_gather x1, waiting for transfers between devices, body(): lax.all_gather(jnp.dot(mixed_low, out_full, preferred_element_type=jnp.fl...  162 us
    psum x1, waiting for transfers between devices, body(): lax.psum(jnp.dot(act_low, down_full, preferred_element_type=jnp.float32)....  102 us
    psum x1, waiting for transfers between devices, body(): lax.psum(hidden_part.astype(jnp.bfloat16), 'mp').astype(jnp.float32)  90.5 us
    dot_general x8, matrix products, scores_at(): jnp.einsum('qhd,khd->hqk', query_block, keys_all, preferred_element_type=...  54.9 us
    psum x1, blocking collectives, body(): lax.psum((padded_qkv, padded_up, out_bias_term, gain_one_term, shift_one_...  44.6 us
    dynamic_update_slice x12, local copies, waits for them, and re-layouts, body(): attended, all_maxima, all_totals = lax.map(attend, jnp.arange(block_count))  38.4 us
    reduce_sum x4, other arithmetic, attend(): totals = jnp.sum(raised, -1, keepdims=True)  27 us
    dot_general x4, matrix products, attend(): jnp.einsum('hqk,khd->qhd', prob_low, values, preferred_element_type=jnp.f...  26.6 us
  transfers between devices with their start and end apart: 8, of which 5 were waited for; matrix products, arithmetic and copies ran while one was open for 21% of the time, Pallas kernels for 0%

profile of v1, /device:TPU:0, one launch (start us, length us, event | category | flops | bytes accessed | tf_op | source)
XLA Modules:
  0.0 869.0 jit_solution(13567843034031352649)
XLA Ops:
  8.2 11.1 %all_gather.19 = bf16[192,640]{0,1:T(8,128)(2,1)S(1)} all-gather(bf16[192,80]{0,1:T(8,128)(2,1)} %param.23), channel_id=1, replica_groups=mesh['dp'=8,'mp'=4] {'dp'}, dimensions={1}, use_global_device_ids=true | all-gather | bytes 276480 | tf_op jit(solution)/shard_map/all_gather | solution.py:62
  19.3 10.8 %all_gather.18 = bf16[3,640,192]{2,1,0:T(8,128)(2,1)S(1)} all-gather(bf16[3,80,192]{2,1,0:T(8,128)(2,1)} %param.21), channel_id=1, replica_groups=mesh['dp'=8,'mp'=4] {'dp'}, dimensions={1}, use_global_device_ids=true | all-gather | bytes 829440 | tf_op jit(solution)/shard_map/all_gather | solution.py:61
  30.2 4.4 fusion.38
  35.3 124.1 %while.29 = (s32[]{:T(128)}, f32[4,512,3,64]{1,0,3,2:T(4,128)}, f32[4,3,512,1]{2,1,3,0:T(4,128)}, f32[4,3,512,1]{2,1,3,0:T(4,128)S(1)}, s32[4]{0:T(128)S(1)}, /*...) while((s32[]{:T(128)}, f32[4,512,3,64]{1,0,3,2:T(4,128)}, ...), condition=%wide.region_3.4_spmd, body=%wide.region_0.3_spmd.sunk | while | flops 844100608 | bytes 45756624 | solution.py:108
  37.3 6.0 fusion.104
  43.3 6.8 fusion.105
  50.1 6.7 fusion.106
  57.8 8.6 dynamic_update_slice.30
  68.4 6.0 fusion.104
  74.4 6.8 fusion.105
  81.1 6.7 fusion.106
  88.8 8.6 dynamic_update_slice.30
  99.4 6.0 fusion.104
  105.4 6.8 fusion.105
  112.1 6.7 fusion.106
  119.8 8.6 dynamic_update_slice.30
  130.4 6.0 fusion.104
  136.4 6.8 fusion.105
  143.2 6.7 fusion.106
  150.9 8.6 dynamic_update_slice.30
  166.4 11.6 %all_gather.22 = bf16[640,560]{1,0:T(8,128)(2,1)} all-gather(bf16[80,560]{1,0:T(8,128)(2,1)S(1)} %copy-done.28), channel_id=1, replica_groups=mesh['dp'=8,'mp'=4] {'dp'}, dimensions={0}, use_global_device_ids=true | all-gather | bytes 806400 | tf_op jit(solution)/shard_map/all_gather | solution.py:63
  178.0 11.1 %all_gather.23 = bf16[560,640]{0,1:T(8,128)(2,1)} all-gather(bf16[560,80]{0,1:T(8,128)(2,1)S(1)} %copy-done.29), channel_id=1, replica_groups=mesh['dp'=8,'mp'=4] {'dp'}, dimensions={1}, use_global_device_ids=true | all-gather | bytes 806400 | tf_op jit(solution)/shard_map/all_gather | solution.py:64
  189.1 161.6 %all-gather.3.cloned.1.call-done = bf16[8192,640]{1,0:T(8,128)(2,1)} async-done(((bf16[2048,640]{1,0:T(8,128)(2,1)}), bf16[8192,640]{1,0:T(8,128)(2,1)}) %all-gather.3.cloned.1.call-update) | async-done | bytes 10485776 | tf_op jit(solution)/shard_map/all_gather | solution.py:117
  350.7 7.3 reduce_sum.219
  363.5 13.4 %multiply_convert_fusion.1 = (bf16[2048,560]{0,1:T(8,128)(2,1)S(1)}, f32[2048,560]{0,1:T(8,128)}, f32[2048,560]{0,1:T(8,128)}) fusion(f32[560]{0:T(1024)S(1)} %copy-done.43, bf16[640,560]{1,0:T(8,128)(2,1)S(1)} %copy-done.22, f32[2048,640]{1,0:T(8,128)S(1)} %subtract_multiply_fusion.3, f32[640]{0:T(1024)S(1)} %copy-done.35, f32[640]{0:T(1024)S(1)} %copy-done.30), kind=kOutput, calls=%fused_computation.61 | convolution fusion | flops 1547632640 | bytes 17435840 | tf_op jit(solution)/shard_map/dot_general | solution.py:127
  378.4 3.9 convolution_convert_fusion.1
  382.5 102.2 %all-reduce.5.cloned.1.call-done = bf16[2048,640]{1,0:T(8,128)(2,1)} async-done(((bf16[2048,640]{1,0:T(8,128)(2,1)}), bf16[2048,640]{1,0:T(8,128)(2,1)}) %all-reduce.5.cloned.1.call-update) | async-done | bytes 2621456 | tf_op jit(solution)/shard_map/psum | solution.py:129
  484.7 4.5 fusion.52
  489.3 3.5 multiply_reduce_fusion.3
  498.7 4.5 convert_reduce_fusion
  504.6 4.0 convolution_convert_fusion
  509.1 5.2 convolution_convert_fusion.5
  516.6 4.2 all-to-all-start.3
  521.3 90.5 %all-reduce.7.cloned.1.call-done = bf16[2048,640]{1,0:T(8,128)(2,1)} async-done(((bf16[2048,640]{1,0:T(8,128)(2,1)}), bf16[2048,640]{1,0:T(8,128)(2,1)}) %all-reduce.7.cloned.1.call-update) | async-done | bytes 2621456 | tf_op jit(solution)/shard_map/psum | solution.py:148
  611.8 6.9 multiply_reduce_fusion.5
  618.8 6.6 fusion.57
  629.0 115.0 %while.30 = (s32[]{:T(128)}, f32[2048,3,64]{0,2,1:T(8,128)S(1)}, f32[2048,3,64]{0,2,1:T(8,128)S(1)}, bf16[4,512,3,64]{1,3,2,0:T(8,128)(2,1)}, s32[4]{0:T(128)S(1...) while((s32[]{:T(128)}, f32[2048,3,64]{0,2,1:T(8,128)S(1)}, ...), condition=%wide.region_17.18_spmd.clone, body=%wide.region_15.17_spmd.clone.sunk | while | flops 2047834624 | bytes 118950256 | solution.py:188
  631.7 3.2 fusion.116
  634.9 7.7 multiply_reduce_fusion.10
  642.6 5.5 multiply_convert_fusion.6
  648.1 6.2 fusion.118
  660.5 3.2 fusion.116
  663.7 7.7 multiply_reduce_fusion.10
  671.4 5.5 multiply_convert_fusion.6
  676.9 6.2 fusion.118
  689.2 3.2 fusion.116
  692.4 7.7 multiply_reduce_fusion.10
  700.1 5.5 multiply_convert_fusion.6
  705.6 6.2 fusion.118
  718.0 3.2 fusion.116
  721.2 7.7 multiply_reduce_fusion.10
  728.9 5.5 multiply_convert_fusion.6
  734.4 6.2 fusion.118
  751.6 4.0 bitcast_convert_fusion
  755.7 4.5 convolution_convert_fusion.4
  761.4 3.8 all-to-all-start.2
  768.2 3.0 dynamic-slice_reduce_fusion
  773.1 5.0 all-to-all-done.2
  779.0 3.0 convolution_convert_fusion.6
  783.8 4.1 all-to-all-start.1
  787.9 5.1 fusion.46
  797.5 4.2 all-to-all-start
  806.7 44.6 %all-reduce = (f32[2,768]{1,0:T(2,128)S(1)}, f32[640]{0:T(1024)}, f32[640]{0:T(1024)}, f32[640]{0:T(1024)}, f32[2240]{0:T(1024)S(1)}, /*index=5*/f32[640]{0:T(1024)}, f32[640]{0:T(1024)}, f32[640]{0:T(1024)}) all-reduce(f32[2,768]{1,0:T(2,128)S(1)} %dynamic_update_slice.20, ...), channel_id=1, replica_groups=mesh['dp'=8,'mp'=4] {'dp','mp'}, use_global_device_ids=true, to_apply=%region_22.23 | all-reduce | flops 7616 | bytes 60928 | tf_op jit(solution)/shard_map/psum | solution.py:226
  856.3 3.5 all-reduce.9.cloned.1.call-done
  (247 shorter events, 94.2 us)
Async XLA Ops:
  7.2 343.5 %all-gather.3.cloned.1.call-start = ((), (), s32[]{:S(2)}) async-start(), calls=%async_computation.7 | async-start | bytes 13107200 | tf_op jit(solution)/shard_map/all_gather | solution.py:117
  7.4 155.0 %copy-start.38 = (f32[192]{0:T(256)}, f32[192]{0:T(256)S(1)}, u32[]{:S(2)}) copy-start(f32[192]{0:T(256)S(1)} %mul.192) | copy-start | bytes 2308
  30.1 4.6 copy-start.20
  159.5 6.8 copy-start.2
  159.5 6.8 copy-start.5
  159.5 6.9 copy-start.14
  159.5 6.9 copy-start.28
  162.4 15.6 %copy-start.29 = (bf16[560,80]{0,1:T(8,128)(2,1)S(1)}, bf16[560,80]{0,1:T(8,128)(2,1)}, u32[]{:S(2)}) copy-start(bf16[560,80]{0,1:T(8,128)(2,1)} %param.29) | copy-start | bytes 268804
  166.3 318.4 %all-reduce.5.cloned.1.call-start = ((), (), s32[]{:S(2)}) async-start(), calls=%async_computation.4 | async-start | bytes 5242880 | tf_op jit(solution)/shard_map/psum | solution.py:129
  350.7 7.3 copy-start.37
  358.0 2.8 copy-start.11
  363.5 13.4 %copy-start = (f32[2048,640]{1,0:T(8,128)}, f32[2048,640]{1,0:T(8,128)S(1)}, u32[]{:S(2)}) copy-start(f32[2048,640]{1,0:T(8,128)S(1)} %subtract_multiply_fusion.3) | copy-start | bytes 15728644
  363.5 14.8 %copy-start.24 = (bf16[560,640]{0,1:T(8,128)(2,1)S(1)}, bf16[560,640]{0,1:T(8,128)(2,1)}, u32[]{:S(2)}) copy-start(bf16[560,640]{0,1:T(8,128)(2,1)} %all_gather.23) | copy-start | bytes 2150404
  376.9 1.4 copy-start.44
  378.4 106.4 %copy-start.34 = (f32[640]{0:T(1024)S(1)}, f32[640]{0:T(1024)}, u32[]{:S(2)}) copy-start(f32[640]{0:T(1024)} %param.30) | copy-start | bytes 7684
  382.3 229.5 %all-reduce.7.cloned.1.call-start = ((), (), s32[]{:S(2)}) async-start(), calls=%async_computation.5 | async-start | bytes 5242880 | tf_op jit(solution)/shard_map/psum | solution.py:148
  484.7 4.6 copy-start.10
  484.7 8.1 slice-start
  489.3 3.6 copy-start.3
  489.3 3.6 copy-start.32
  489.3 4.5 slice-start.1
  489.3 9.3 %slice-start.2 = ((s8[4587520]{0:T(1024)(128)(4,1)}), s8[4194304]{0:T(1024)(128)(4,1)S(1)}, s32[]{:S(2)}) async-start(s8[4587520]{0:T(1024)(128)(4,1)} %bitcast.143), calls=%async_computation.10 | async-start | bytes 8388608
  489.3 9.3 %slice-start.4 = ((s8[4587520]{0:T(1024)(128)(4,1)}), s8[4194304]{0:T(1024)(128)(4,1)S(1)}, s32[]{:S(2)}) async-start(s8[4587520]{0:T(1024)(128)(4,1)} %bitcast.145), calls=%async_computation.12 | async-start | bytes 8388608
  493.9 4.8 slice-start.3
  493.9 4.8 slice-start.5
  496.3 2.3 copy-start.1
  498.6 4.6 copy-start.13
  498.7 5.9 copy-start.23
  516.6 244.8 %all-to-all-start.3 = ((bf16[8,560,80]{1,2,0:T(8,128)(2,1)}), bf16[8,560,80]{1,2,0:T(8,128)(2,1)}, u32[]{:S(2)}, u32[]{:S(2)}) async-start(bf16[8,560,80]{1,2,0:T(8,128)(2,1)} %bitcast.132), calls=%async_computation.3 | async-start | bytes 1638400 | tf_op jit(solution)/shard_map/all_to_all | solution.py:19
  520.8 339.0 %all-reduce.9.cloned.1.call-start = ((), (), s32[]{:S(2)}) async-start(), calls=%async_computation.6 | async-start | bytes 5242880 | tf_op jit(solution)/shard_map/psum | solution.py:203
  618.8 6.6 copy-start.9
  618.8 9.2 %copy-start.42 = (bf16[3]{0:T(256)(128)(2,1)S(1)}, bf16[3]{0:T(256)(128)(2,1)}, u32[]{:S(2)}) copy-start(bf16[3]{0:T(256)(128)(2,1)} %fusion.55) | copy-start | bytes 22
  625.4 1.5 copy-start.7
  631.7 3.2 copy-start.6
  631.7 3.2 copy-start.15
  648.1 6.2 copy-start.25
  656.3 1.4 copy-start.26
  660.5 3.2 copy-start.6
  660.5 3.2 copy-start.15
  676.9 6.2 copy-start.25
  685.1 1.4 copy-start.26
  689.2 3.2 copy-start.6
  689.2 3.2 copy-start.15
  705.6 6.2 copy-start.25
  713.8 1.4 copy-start.26
  717.9 3.2 copy-start.6
  718.0 3.2 copy-start.15
  734.4 6.2 copy-start.25
  742.6 1.4 copy-start.26
  749.6 1.4 copy-start.16
  749.6 2.0 copy-start.21
  751.6 4.0 copy-start.31
  751.6 4.0 copy-start.36
  751.6 4.1 copy-start.46
  760.1 5.1 copy-start.4
  761.4 6.5 copy-start.41
  761.4 6.8 copy-start.33
  761.4 6.8 copy-start.40
  761.4 16.8 %all-to-all-start.2 = ((bf16[8,80,560]{2,1,0:T(8,128)(2,1)}), bf16[8,80,560]{2,1,0:T(8,128)(2,1)S(1)}, u32[]{:S(2)}, u32[]{:S(2)}) async-start(bf16[8,80,560]{2,1,0:T(8,128)(2,1)} %bitcast.22), calls=%async_computation.2 | async-start | bytes 1638400 | tf_op jit(solution)/shard_map/all_to_all | solution.py:19
  767.8 11.1 %copy-start.8 = (bf16[2048,640]{1,0:T(8,128)(2,1)S(1)}, bf16[2048,640]{1,0:T(8,128)(2,1)}, u32[]{:S(2)}) copy-start(bf16[2048,640]{1,0:T(8,128)(2,1)} %copy-done.7) | copy-start | bytes 7864324
  767.8 11.1 %copy-start.39 = (f32[192]{0:T(256)S(1)}, f32[192]{0:T(256)}, u32[]{:S(2)}) copy-start(f32[192]{0:T(256)} %copy-done.38) | copy-start | bytes 2308
  779.0 8.9 %copy-start.17 = (bf16[1,2048,192]{1,2,0:T(8,128)(2,1)S(1)}, bf16[1,2048,192]{1,2,0:T(8,128)(2,1)}, u32[]{:S(2)}) copy-start(bf16[1,2048,192]{1,2,0:T(8,128)(2,1)} %stack.24) | copy-start | bytes 2359300
  783.8 13.7 %all-to-all-start.1 = ((bf16[8,192,80]{1,2,0:T(8,128)(2,1)}), bf16[8,192,80]{1,2,0:T(8,128)(2,1)}, u32[]{:S(2)}, u32[]{:S(2)}) async-start(bf16[8,192,80]{1,2,0:T(8,128)(2,1)} %bitcast.138), calls=%async_computation.1 | async-start | bytes 655360 | tf_op jit(solution)/shard_map/all_to_all | solution.py:19
  797.5 56.7 %all-to-all-start = ((bf16[8,3,80,192]{3,2,1,0:T(8,128)(2,1)}), bf16[8,3,80,192]{3,2,1,0:T(8,128)(2,1)}, u32[]{:S(2)}, u32[]{:S(2)}) async-start(bf16[8,3,80,192]{3,2,1,0:T(8,128)(2,1)} %copy.39), calls=%async_computation | async-start | bytes 1966080 | tf_op jit(solution)/shard_map/all_to_all | solution.py:19
  (9 other events, 9.8 us)
Sparse Core Ops, SparseCore 0:
  166.4 184.2 all-gather.2
  382.4 102.2 all-reduce.4
  508.6 103.1 all-reduce.6
  755.7 104.0 all-reduce.8
